TPU v7x, 256 devices: a whole 4x4x8 slice. The times are simulated.
256 devices in a mesh: ctx: 64 (over y, x, z_lo, core), grp: 4 (over z_hi).
Axes of the slice: x: 4, y: 4, z: 8 (z_hi: 4, z_lo: 2; z = z_hi * 2 + z_lo), core: 2. Of those that a mesh axis runs over, the one named last changes fastest.
Arguments:
- saved_input: bfloat16 [4, 2048, 8192], P('grp', None, 'ctx'), may hold values from -6 to 6
- out_grad: bfloat16 [4, 2048, 8192], P('grp', None, 'ctx'), may hold values from -0.0625 to 0.0625
- filters: float32 [4, 2048, 8192], P('grp', 'ctx'), may hold values from -6 to 6
- adapter_down: bfloat16 [16, 4, 2048], P(None, 'grp'), may hold values from -0.0625 to 0.0625
- adapter_up: bfloat16 [16, 4, 2048], P(None, 'grp'), may hold values from -0.25 to 0.25
Outputs:
- grad_input: bfloat16 [4, 2048, 8192], P('grp', None, 'ctx')
- grad_filter: float32 [4, 2048, 8192], P('grp', 'ctx')
- grad_down: float32 [16, 4, 2048], P(None, 'grp')
- grad_up: float32 [16, 4, 2048], P(None, 'grp')
All inputs are finite; a program needn't handle non-finite values.
Results may differ from a plain program's by a relative error of at most 0.0075.
Values may be sent and summed in bfloat16 or wider, within the bound.
A program may use at most 64 MiB of HBM per device.

v0:
```python
import math

import jax
import jax.numpy as jnp
from jax import lax
from jax.sharding import PartitionSpec as P

HIGH = lax.Precision.HIGHEST


def split_radix(points):
    radix_low = 1
    while (
        points % (radix_low * 2) == 0
        and radix_low * 2 * (radix_low * 2) <= points
        and (points // (radix_low * 2) % 2 == 0)
    ):
        radix_low = radix_low * 2
    return (radix_low, points // radix_low)


def angle_table(height, across, period):
    index_down = lax.broadcasted_iota(jnp.int32, (height, across), 0)
    index_across = lax.broadcasted_iota(jnp.int32, (height, across), 1)
    phase = (index_down * index_across % period).astype(jnp.float32) * (2.0 * math.pi / period)
    return (jnp.cos(phase), jnp.sin(phase))


def make_tables(points):
    radix_low, radix_high = split_radix(points)
    cos_one, sin_one = angle_table(radix_high, radix_high // 2, radix_high)
    first = jnp.concatenate([cos_one, -sin_one], axis=0)
    first_high = first.astype(jnp.bfloat16)
    first_low = (first - first_high.astype(jnp.float32)).astype(jnp.bfloat16)
    twist = angle_table(radix_high, radix_low, points)
    cos_two, sin_two = angle_table(radix_low, radix_low, radix_low)
    second_fwd = jnp.concatenate(
        [jnp.concatenate([cos_two, sin_two], axis=1), jnp.concatenate([-sin_two, cos_two], axis=1)],
        axis=0,
    )
    second_inv = jnp.concatenate(
        [jnp.concatenate([cos_two, -sin_two], axis=1), jnp.concatenate([sin_two, cos_two], axis=1)],
        axis=0,
    )
    last_inv = jnp.concatenate([cos_one, -sin_one], axis=0)
    return (
        radix_low,
        radix_high,
        first,
        first_high,
        first_low,
        twist,
        second_fwd,
        second_inv,
        last_inv,
    )


def forward_dft(signal, tables):
    radix_low, radix_high, first, first_high, first_low, twist, second_fwd, second_inv, last_inv = (
        tables
    )
    channels = signal.shape[0]
    blocks = signal.reshape(channels, radix_high // 2, radix_low)
    if signal.dtype == jnp.bfloat16:
        section_one = jnp.einsum(
            "kn,cnp->ckp", first_high, blocks, preferred_element_type=jnp.float32
        )
        section_one = section_one + jnp.einsum(
            "kn,cnp->ckp", first_low, blocks, preferred_element_type=jnp.float32
        )
    else:
        section_one = jnp.einsum("kn,cnp->ckp", first, blocks, precision=HIGH)
    real_one = section_one[:, :radix_high]
    imag_one = section_one[:, radix_high:]
    cos_twist, sin_twist = twist
    real_two = real_one * cos_twist + imag_one * sin_twist
    imag_two = imag_one * cos_twist - real_one * sin_twist
    joined = jnp.concatenate([real_two, imag_two], axis=2)
    spectrum = jnp.einsum("jq,ckq->cjk", second_fwd, joined, precision=HIGH)
    return (spectrum[:, :radix_low], spectrum[:, radix_low:])


def inverse_dft(spectrum, tables):
    radix_low, radix_high, first, first_high, first_low, twist, second_fwd, second_inv, last_inv = (
        tables
    )
    spec_real, spec_imag = spectrum
    channels = spec_real.shape[0]
    joined = jnp.concatenate([spec_real, spec_imag], axis=1)
    section_one = jnp.einsum("pq,cqk->cpk", second_inv, joined, precision=HIGH)
    real_one = section_one[:, :radix_low]
    imag_one = section_one[:, radix_low:]
    cos_twist = twist[0].T
    sin_twist = twist[1].T
    real_two = real_one * cos_twist - imag_one * sin_twist
    imag_two = real_one * sin_twist + imag_one * cos_twist
    stacked = jnp.concatenate([real_two, imag_two], axis=2)
    signal = jnp.einsum("kn,cpk->cnp", last_inv, stacked, precision=HIGH)
    return signal.reshape(channels, -1) / float(radix_low * radix_high)


def conj_product(spec_left, spec_right):
    left_real, left_imag = spec_left
    right_real, right_imag = spec_right
    return (
        left_real * right_real + left_imag * right_imag,
        left_imag * right_real - left_real * right_imag,
    )


def body(saved_input, out_grad, filters, adapter_down, adapter_up):
    tok_input = saved_input[0]
    tok_grad = out_grad[0]
    down_rows = adapter_down[:, 0, :]
    up_float = adapter_up[:, 0, :].astype(jnp.float32)
    rank_part = jnp.dot(down_rows, tok_input, preferred_element_type=jnp.float32)
    rank_acts = lax.psum(rank_part, "grp")
    tok_act = (
        tok_input.astype(jnp.float32) + jnp.einsum("rc,rt->ct", up_float, rank_acts, precision=HIGH)
    ).astype(jnp.bfloat16)
    chan_act, chan_grad = (
        lax.all_to_all(tok_act, "ctx", split_axis=0, concat_axis=1, tiled=True),
        lax.all_to_all(tok_grad, "ctx", split_axis=0, concat_axis=1, tiled=True),
    )
    length = chan_act.shape[1]
    tables = make_tables(2 * length)
    act_spec = forward_dft(chan_act, tables)
    grad_spec = forward_dft(chan_grad, tables)
    kern_spec = forward_dft(filters[0], tables)
    chan_du = inverse_dft(conj_product(grad_spec, kern_spec), tables).astype(jnp.bfloat16)
    filt_grad = inverse_dft(conj_product(grad_spec, act_spec), tables)
    tok_du = lax.all_to_all(chan_du, "ctx", split_axis=1, concat_axis=0, tiled=True)
    du_float = tok_du.astype(jnp.float32)
    rank_grad = lax.psum(jnp.einsum("rc,ct->rt", up_float, du_float, precision=HIGH), "grp")
    grad_input = (
        du_float + jnp.einsum("rc,rt->ct", down_rows.astype(jnp.float32), rank_grad, precision=HIGH)
    ).astype(jnp.bfloat16)
    down_part = jnp.einsum("rt,ct->rc", rank_grad, tok_input.astype(jnp.float32), precision=HIGH)
    up_part = jnp.einsum("rt,ct->rc", rank_acts, du_float, precision=HIGH)
    down_sum, up_sum = lax.psum((down_part, up_part), "ctx")
    factor = float(length) ** (-0.5)
    return (
        grad_input[None],
        filt_grad[None],
        (factor * down_sum)[:, None, :],
        (factor * up_sum)[:, None, :],
    )


def solution(mesh):
    placed = (
        P("grp", None, "ctx"),
        P("grp", None, "ctx"),
        P("grp", "ctx", None),
        P(None, "grp", None),
        P(None, "grp", None),
    )
    return jax.shard_map(
        body,
        mesh=mesh,
        in_specs=placed,
        out_specs=(
            P("grp", None, "ctx"),
            P("grp", "ctx", None),
            P(None, "grp", None),
            P(None, "grp", None),
        ),
        check_vma=False,
    )
```

profile of v0, /device:TPU:1, one launch (start us, length us, event | category | flops | bytes accessed | tf_op | source)
XLA Modules:
  0.0 635.6 jit_solution(4558372713880464864)
XLA Ops:
  7.2 10.5 %all-to-all-start = ((bf16[64,32,128]{2,1,0:T(8,128)(2,1)}), bf16[64,32,128]{2,1,0:T(8,128)(2,1)S(1)}, u32[]{:S(2)}, u32[]{:S(2)}) async-start(bf16[64,32,128]{2,1,0:T(8,128)(2,1)} %bitcast.118), calls=%async_computation | async-start | bytes 1048576 | tf_op jit(solution)/shard_map/all_to_all | solution.py:124
  17.7 1.4 copy.58
  20.5 5.2 convolution_bitcast_fusion.2
  25.7 4.7 all-to-all-done
  32.0 1.4 copy-done.4
  33.4 1.3 multiply_add_fusion.6
  34.7 7.3 %fusion.45 = f32[32,256,128]{1,2,0:T(8,128)S(1)} fusion(f32[32,128,128]{1,2,0:T(8,128)S(1)} %get-tuple-element.31, f32[32,128,128]{1,2,0:T(8,128)S(1)} %get-tuple-element.30, f32[128,128]{1,0:T(8,128)S(1)} %get-tuple-element.39, f32[128,128]{1,0:T(8,128)S(1)} %fusion.119, f32[128,128]{1,0:T(8,128)S(1)} %get-tuple-element.38), kind=kOutput, calls=%fused_computation.41 | convolution fusion | flops 3222470656 | bytes 8585216 | tf_op jit(solution)/shard_map/jq,ckq->cjk/dot_general | solution.py:80
  42.0 7.5 %fusion.42 = f32[32,256,128]{1,2,0:T(8,128)S(1)} fusion(f32[32,128,128]{1,2,0:T(8,128)S(1)} %get-tuple-element.34, f32[32,128,128]{1,2,0:T(8,128)S(1)} %get-tuple-element.35, f32[128,128]{1,0:T(8,128)S(1)} %get-tuple-element.39, f32[128,128]{1,0:T(8,128)S(1)} %fusion.119, f32[128,128]{1,0:T(8,128)S(1)} %get-tuple-element.38), kind=kOutput, calls=%fused_computation.40 | convolution fusion | flops 3222470656 | bytes 8585216 | tf_op jit(solution)/shard_map/jq,ckq->cjk/dot_general | solution.py:80
  50.1 3.5 fusion.39
  54.2 2.9 fusion.60
  57.1 1.1 copy.43
  58.3 4.5 all-to-all-start.1
  63.3 12.4 %all-to-all-done.1 = bf16[32,64,128]{2,0,1:T(8,128)(2,1)S(1)} async-done(((bf16[32,64,128]{2,0,1:T(8,128)(2,1)}), bf16[32,64,128]{2,0,1:T(8,128)(2,1)S(1)}, u32[]{:S(2)}, u32[]{:S(2)}) %all-to-all-start.1) | async-done | bytes 524320 | tf_op jit(solution)/shard_map/all_to_all | solution.py:133
  75.9 17.6 %all-reduce.1 = (f32[16,128]{1,0:T(8,128)S(1)}, f32[16,128]{1,0:T(8,128)S(1)}) all-reduce(f32[16,128]{1,0:T(8,128)S(1)} %convolution_bitcast_fusion.3, f32[16,128]{1,0:T(8,128)S(1)} %fusion.65), channel_id=1, replica_groups=mesh['ctx'=64,'grp'=4] {'grp'}, use_global_device_ids=true, to_apply=%region_0.0 | all-reduce | flops 4096 | bytes 32768 | tf_op jit(solution)/shard_map/psum | solution.py:135
  93.5 1.2 fusion.130
  94.6 1.2 fusion.63
  96.7 1.0 copy.46
  97.7 8.5 %all-to-all-start.2 = ((bf16[64,32,128]{2,1,0:T(8,128)(2,1)}), bf16[64,32,128]{2,1,0:T(8,128)(2,1)S(1)}, u32[]{:S(2)}, u32[]{:S(2)}) async-start(bf16[64,32,128]{2,1,0:T(8,128)(2,1)} %bitcast.26), calls=%async_computation.2 | async-start | bytes 1048576 | tf_op jit(solution)/shard_map/all_to_all | solution.py:123
  106.8 1.0 copy.50
  107.8 498.9 %all-reduce.4.cloned.1.call-done = (f32[16,2048]{1,0:T(8,128)}, f32[16,2048]{1,0:T(8,128)}) async-done(((f32[16,2048]{1,0:T(8,128)}, f32[16,2048]{1,0:T(8,128)}), (f32[16,2048]{1,0:T(8,128)}, f32[16,2048]{1,0:T(8,128)})) %all-reduce.4.cloned.1.call-update) | async-done | bytes 262160 | tf_op jit(solution)/shard_map/psum | solution.py:141
  612.3 7.1 %fusion.36 = f32[32,256,128]{1,2,0:T(8,128)S(1)} fusion(f32[32,128,128]{1,2,0:T(8,128)S(1)} %get-tuple-element.27, f32[32,128,128]{1,2,0:T(8,128)S(1)} %get-tuple-element.26, f32[128,128]{1,0:T(8,128)S(1)} %get-tuple-element.39, f32[128,128]{1,0:T(8,128)S(1)} %fusion.119, f32[128,128]{1,0:T(8,128)S(1)} %get-tuple-element.38), kind=kOutput, calls=%fused_computation.38 | convolution fusion | flops 3222470656 | bytes 8585216 | tf_op jit(solution)/shard_map/jq,ckq->cjk/dot_general | solution.py:80
  620.1 3.8 fusion.33
  624.5 2.9 fusion.51
  627.4 1.2 div.13
  (42 shorter events, 13.1 us)
Async XLA Ops:
  7.2 68.5 %copy-start = (bf16[16,1,2048]{2,0,1:T(8,128)(2,1)S(1)}, bf16[16,1,2048]{2,0,1:T(8,128)(2,1)}, u32[]{:S(2)}) copy-start(bf16[16,1,2048]{2,0,1:T(8,128)(2,1)} %param.9) | copy-start | bytes 196612
  7.2 23.2 %all-to-all-start = ((bf16[64,32,128]{2,1,0:T(8,128)(2,1)}), bf16[64,32,128]{2,1,0:T(8,128)(2,1)S(1)}, u32[]{:S(2)}, u32[]{:S(2)}) async-start(bf16[64,32,128]{2,1,0:T(8,128)(2,1)} %bitcast.118), calls=%async_computation | async-start | bytes 1048576 | tf_op jit(solution)/shard_map/all_to_all | solution.py:124
  31.2 2.2 copy-start.4
  42.0 7.5 %copy-start.2 = (f32[32,256,128]{1,2,0:T(8,128)}, f32[32,256,128]{1,2,0:T(8,128)S(1)}, u32[]{:S(2)}) copy-start(f32[32,256,128]{1,2,0:T(8,128)S(1)} %fusion.45) | copy-start | bytes 12582916
  57.1 5.8 copy-start.5
  57.1 6.0 copy-start.6
  58.3 17.4 %all-to-all-start.1 = ((bf16[32,64,128]{2,0,1:T(8,128)(2,1)}), bf16[32,64,128]{2,0,1:T(8,128)(2,1)S(1)}, u32[]{:S(2)}, u32[]{:S(2)}) async-start(bf16[32,64,128]{2,0,1:T(8,128)(2,1)} %copy.43), calls=%async_computation.1 | async-start | bytes 1048576 | tf_op jit(solution)/shard_map/all_to_all | solution.py:133
  62.8 543.9 %all-reduce.4.cloned.1.call-start = ((), (), s32[]{:S(2)}) async-start(), calls=%async_computation.3 | async-start | bytes 524288 | tf_op jit(solution)/shard_map/psum | solution.py:141
  97.7 512.5 %all-to-all-start.2 = ((bf16[64,32,128]{2,1,0:T(8,128)(2,1)}), bf16[64,32,128]{2,1,0:T(8,128)(2,1)S(1)}, u32[]{:S(2)}, u32[]{:S(2)}) async-start(bf16[64,32,128]{2,1,0:T(8,128)(2,1)} %bitcast.26), calls=%async_computation.2 | async-start | bytes 1048576 | tf_op jit(solution)/shard_map/all_to_all | solution.py:123
  612.3 7.1 %copy-start.3 = (f32[32,256,128]{1,2,0:T(8,128)S(1)}, f32[32,256,128]{1,2,0:T(8,128)}, u32[]{:S(2)}) copy-start(f32[32,256,128]{1,2,0:T(8,128)} %copy-done.2) | copy-start | bytes 12582916
  624.5 4.0 copy-start.1
Sparse Core Ops, SparseCore 0:
  96.0 510.7 all-reduce.3
where the time goes:
time: 640 us; the launch traced here: 636 us
  waiting for transfers between devices  516 us (81%)
  matrix products  47.1 us (7%)
  starting transfers between devices  23.5 us (4%)
  blocking collectives  17.6 us (3%)
  between operations  14.6 us (2%)
  local copies, waits for them, and re-layouts  9.35 us (1%)
  other arithmetic  7.43 us (1%)
    psum x1, waiting for transfers between devices, body(): down_sum, up_sum = lax.psum((down_part, up_part), 'ctx')  499 us
    dot_general x3, matrix products, forward_dft(): spectrum = jnp.einsum('jq,ckq->cjk', second_fwd, joined, precision=HIGH)  21.9 us
    psum x1, blocking collectives, body(): lax.psum(jnp.einsum('rc,ct->rt', up_float, du_float, precision=HIGH), 'grp')  17.6 us
  transfers between devices with their start and end apart: 4, of which 3 were waited for; matrix products, arithmetic and copies ran while one was open for 2% of the time, Pallas kernels for 0%

commit v1 on v0

v1 whole, which is shorter than its diff:
```python
import functools
import math

import jax
import jax.numpy as jnp
import numpy as np
from jax import lax
from jax.experimental import pallas as pl
from jax.experimental.pallas import tpu as pltpu
from jax.sharding import PartitionSpec as P

MESH = pl.DeviceIdType.MESH
F32 = jnp.float32
BF16 = jnp.bfloat16
LANES = 128
CHANS = 32
STEP = 8
GRID = {64: (4, 4, 2, 2), 8: (2, 2, 2, 1)}
SCRAMBLE = 29


def halves(table):
    high = table.astype(BF16)
    low = (table - high.astype(np.float64)).astype(BF16)
    return high, low


def make_tables(rows):
    points = 2 * rows * LANES
    n = np.arange(rows)
    p = np.arange(LANES)
    theta = np.outer(n + 0.5, n) * (2.0 * math.pi / (2 * rows))
    phi = np.outer(p, p) * (2.0 * math.pi / LANES)
    turn = np.outer(n + 0.5, p) * (2.0 * math.pi / points)
    high, low = halves(np.concatenate([np.cos(theta), -np.sin(theta)], axis=0))
    first_two = np.concatenate([high, low], axis=1)
    first_three = np.concatenate([high, high, low], axis=1)
    cos, sin = np.cos(phi), np.sin(phi)
    high, low = halves(np.block([[cos, -sin], [sin, cos]]))
    second = np.concatenate([high, high, low], axis=0)
    high, low = halves(np.block([[cos, sin], [-sin, cos]]))
    third = np.concatenate([high, high, low], axis=0)
    high, low = halves(np.concatenate([np.cos(theta).T, -np.sin(theta).T], axis=1) * (2.0 / points))
    last = np.concatenate([high, high, low], axis=1)
    twist = np.stack([np.cos(turn), np.sin(turn)]).astype(np.float32)
    return first_two, first_three, twist, second, third, last


def split(value):
    high = value.astype(BF16)
    return high, (value - high.astype(F32)).astype(BF16)


def dot(left, right, dims=((1,), (0,))):
    return lax.dot_general(left, right, (dims, ((), ())), preferred_element_type=F32)


def gather_rows(ref, first, rows):
    blocks = [ref[pl.ds(first + j, rows, stride=CHANS), :] for j in range(STEP)]
    return jnp.concatenate(blocks, axis=1)


def forward(data, first, twist, second, exact):
    rows = data.shape[0]
    if exact:
        narrow = data.astype(BF16)
        stacked = jnp.concatenate([narrow, narrow], axis=0)
    else:
        high, low = split(data)
        stacked = jnp.concatenate([high, low, high], axis=0)
    part = dot(first[...], stacked)
    cos, sin = twist[0], twist[1]
    joined = []
    for j in range(STEP):
        lanes = slice(j * LANES, (j + 1) * LANES)
        real, imag = part[:rows, lanes], part[rows:, lanes]
        joined.append(jnp.concatenate([real * cos + imag * sin, imag * cos - real * sin], axis=1))
    high, low = split(jnp.concatenate(joined, axis=0))
    return dot(jnp.concatenate([high, low, high], axis=1), second[...])


def inverse(spectrum, twist, third, last):
    rows = twist.shape[1]
    high, low = split(spectrum)
    part = dot(jnp.concatenate([high, low, high], axis=1), third[...])
    cos, sin = twist[0], twist[1]
    reals, imags = [], []
    for j in range(STEP):
        real = part[j * rows : (j + 1) * rows, :LANES]
        imag = part[j * rows : (j + 1) * rows, LANES:]
        reals.append(real * cos - imag * sin)
        imags.append(real * sin + imag * cos)
    joined = jnp.concatenate([jnp.concatenate(reals, axis=1), jnp.concatenate(imags, axis=1)], axis=0)
    high, low = split(joined)
    return dot(last[...], jnp.concatenate([high, low, high], axis=0))


def conj_product(left, right):
    lr, li = left[:, :LANES], left[:, LANES:]
    rr, ri = right[:, :LANES], right[:, LANES:]
    return jnp.concatenate([lr * rr + li * ri, li * rr - lr * ri], axis=1)


def kernel(
    count, groups, factor,
    x_hbm, dy_hbm, h_hbm, a_ref, b_ref, first_two, first_three, twist, second, third, last,
    gi_hbm, gf_hbm, gd_ref, gu_ref,
    x_buf, h_buf, u_buf, du_buf, gi_buf, dy_got, u_got, du_got, wide, work, gf_buf,
    spec_h, spec_dy, z_mine, z_got, r_mine, r_got, parts, part_got, total, total_got,
    load_sem, send_sem, recv_sem,
):
    me = lax.axis_index("ctx")
    grp = lax.axis_index("grp")
    sizes = GRID[count]
    coords, rest = [], me
    for size in reversed(sizes):
        coords.append(rest % size)
        rest = rest // size
    width = count * CHANS

    def peer_of(d):
        rest, stride, peer = (d * SCRAMBLE) % count, 1, 0
        for size, own in zip(reversed(sizes), coords):
            peer = peer + ((own + rest % size) % size) * stride
            rest = rest // size
            stride = stride * size
        return peer

    def each_peer(action):
        def run(d, carry):
            action(peer_of(d))
            return carry

        lax.fori_loop(1, count, run, 0)

    def each_group(action):
        for e in range(1, groups):
            action(lax.rem(grp + e, groups))

    def send(src, dst, slot, target):
        pltpu.make_async_remote_copy(
            src_ref=src, dst_ref=dst, send_sem=send_sem.at[slot], recv_sem=recv_sem.at[slot],
            device_id=target, device_id_type=MESH,
        ).start()

    def wait_for(sems, slot, ref):
        pltpu.make_async_copy(ref, ref, sems.at[slot]).wait()

    barrier = pltpu.get_barrier_semaphore()

    def greet(target):
        pl.semaphore_signal(barrier, inc=1, device_id=target, device_id_type=MESH)

    each_peer(lambda p: greet({"ctx": p}))
    each_group(lambda g: greet({"grp": g}))

    x_load = pltpu.make_async_copy(x_hbm, x_buf, load_sem.at[0])
    x_load.start()

    def load_h(n, carry):
        lanes = pl.ds(pl.multiple_of(n * LANES, LANES), LANES)
        rows = pl.ds(pl.multiple_of(n * CHANS, CHANS), CHANS)
        pltpu.make_async_copy(h_hbm.at[:, lanes], h_buf.at[rows], load_sem.at[1]).start()
        return carry

    lax.fori_loop(0, count, load_h, 0)
    own_rows = pl.ds(pl.multiple_of(me * CHANS, CHANS), CHANS)
    own_dy = pltpu.make_async_copy(dy_hbm.at[own_rows], dy_got.at[me], load_sem.at[2])
    own_dy.start()
    x_load.wait()
    z_part = dot(a_ref[...], x_buf[...])
    z_mine[...] = z_part
    pl.semaphore_wait(barrier, count - 1 + groups - 1)

    each_group(lambda g: send(z_mine, z_got.at[grp], 0, {"grp": g}))

    def send_dy(p):
        rows = pl.ds(pl.multiple_of(p * CHANS, CHANS), CHANS)
        send(dy_hbm.at[rows], dy_got.at[me], 1, {"ctx": p})

    each_peer(send_dy)

    pltpu.make_async_copy(h_buf, h_buf, load_sem.at[1]).wait()

    def spectrum_h(i, carry):
        data = gather_rows(h_buf, i * STEP, count)
        spec_h[pl.ds(pl.multiple_of(i * STEP * count, STEP * count), STEP * count), :] = forward(
            data, first_three, twist, second, False
        )
        return carry

    lax.fori_loop(0, CHANS // STEP, spectrum_h, 0)

    def shared_sum(mine, got):
        got[grp] = mine[...]
        acc = got[0]
        for g in range(1, groups):
            acc = acc + got[g]
        return acc

    def low_rank(base, maps, value, out):
        high, low = split(value)
        pair = jnp.concatenate([high, low], axis=0)
        chunk = 256
        for start in range(0, width, chunk):
            left = maps[:, start : start + chunk]
            left = jnp.concatenate([left, left], axis=0)
            low_part = dot(left, pair, ((0,), (0,)))
            out[start : start + chunk, :] = (base(start, chunk).astype(F32) + low_part).astype(BF16)

    wait_for(recv_sem, 0, z_got.at[pl.ds(0, groups - 1)])
    z = shared_sum(z_mine, z_got)
    low_rank(lambda s, n: x_buf[s : s + n, :], b_ref, z, u_buf)
    u_got[me] = u_buf[own_rows, :]

    def send_u(p):
        rows = pl.ds(pl.multiple_of(p * CHANS, CHANS), CHANS)
        send(u_buf.at[rows], u_got.at[me], 2, {"ctx": p})

    each_peer(send_u)

    others = pl.ds(0, count - 1)
    own_dy.wait()
    wait_for(recv_sem, 1, dy_got.at[others])

    def widen(got):
        def run(n, carry):
            rows = pl.ds(pl.multiple_of(n * CHANS, CHANS), CHANS)
            wide[rows, :] = got[n].astype(F32)
            return carry

        lax.fori_loop(0, count, run, 0, unroll=8)

    def scatter_rows(ref, first, value):
        for j in range(STEP):
            ref[pl.ds(first + j, count, stride=CHANS), :] = value[:, j * LANES : (j + 1) * LANES]

    widen(dy_got)

    def conv_grad(i, carry):
        rows = pl.ds(pl.multiple_of(i * STEP * count, STEP * count), STEP * count)
        spec = forward(gather_rows(wide, i * STEP, count), first_two, twist, second, True)
        spec_dy[rows, :] = spec
        scatter_rows(work, i * STEP, inverse(conj_product(spec, spec_h[rows, :]), twist, third, last))
        return carry

    lax.fori_loop(0, CHANS // STEP, conv_grad, 0)
    def narrow(n, carry):
        rows = pl.ds(pl.multiple_of(n * CHANS, CHANS), CHANS)
        du_buf[rows, :] = work[rows, :].astype(BF16)
        return carry

    lax.fori_loop(0, count, narrow, 0, unroll=8)
    du_got[own_rows, :] = du_buf[own_rows, :]

    def send_du(p):
        rows = pl.ds(pl.multiple_of(p * CHANS, CHANS), CHANS)
        send(du_buf.at[rows], du_got.at[own_rows], 3, {"ctx": p})

    each_peer(send_du)

    wait_for(recv_sem, 2, u_got.at[others])
    widen(u_got)

    def filter_grad(i, carry):
        rows = pl.ds(pl.multiple_of(i * STEP * count, STEP * count), STEP * count)
        spec = forward(gather_rows(wide, i * STEP, count), first_two, twist, second, True)
        scatter_rows(gf_buf, i * STEP, inverse(conj_product(spec_dy[rows, :], spec), twist, third, last))
        return carry

    lax.fori_loop(0, CHANS // STEP, filter_grad, 0)

    def store_gf(n, carry):
        lanes = pl.ds(pl.multiple_of(n * LANES, LANES), LANES)
        rows = pl.ds(pl.multiple_of(n * CHANS, CHANS), CHANS)
        pltpu.make_async_copy(gf_buf.at[rows], gf_hbm.at[:, lanes], load_sem.at[3]).start()
        return carry

    lax.fori_loop(0, count, store_gf, 0)

    wait_for(recv_sem, 3, du_got.at[pl.ds(0, width - CHANS)])
    r_mine[...] = dot(b_ref[...], du_got[...])
    each_group(lambda g: send(r_mine, r_got.at[grp], 4, {"grp": g}))

    ranks = z_mine.shape[0]
    blocks = width // LANES

    def outer(value, tokens, offset):
        high, low = split(value)
        both = dot(jnp.concatenate([high, low], axis=0), tokens, ((1,), (1,)))
        out = (both[:ranks] + both[ranks:]) * factor
        for r in range(ranks // 8):
            for k in range(blocks):
                parts[offset + r * blocks + k] = out[r * 8 : r * 8 + 8, k * LANES : (k + 1) * LANES]

    outer(z, du_got[...], count // 2)
    wait_for(recv_sem, 4, r_got.at[pl.ds(0, groups - 1)])
    rank_grad = shared_sum(r_mine, r_got)
    outer(rank_grad, x_buf[...], 0)
    each_peer(lambda p: send(parts.at[p], part_got.at[me], 5, {"ctx": p}))
    part_got[me] = parts[me]
    low_rank(lambda s, n: du_got[s : s + n, :], a_ref, rank_grad, gi_buf)
    gi_store = pltpu.make_async_copy(gi_buf, gi_hbm, load_sem.at[4])
    gi_store.start()

    wait_for(recv_sem, 5, part_got.at[others])
    acc = jnp.sum(part_got[...], axis=0)
    total[...] = acc
    total_got[me] = acc
    each_peer(lambda p: send(total, total_got.at[me], 6, {"ctx": p}))
    wait_for(recv_sem, 6, total_got.at[others])
    for r in range(ranks // 8):
        for k in range(blocks):
            rows, lanes = slice(r * 8, r * 8 + 8), slice(k * LANES, (k + 1) * LANES)
            gd_ref[rows, lanes] = total_got[r * blocks + k]
            gu_ref[rows, lanes] = total_got[count // 2 + r * blocks + k]

    gi_store.wait()
    pltpu.make_async_copy(gf_buf, gf_buf, load_sem.at[3]).wait()
    wait_for(send_sem, 0, z_got.at[pl.ds(0, groups - 1)])
    wait_for(send_sem, 1, dy_got.at[others])
    wait_for(send_sem, 2, u_got.at[others])
    wait_for(send_sem, 3, du_got.at[pl.ds(0, width - CHANS)])
    wait_for(send_sem, 4, r_got.at[pl.ds(0, groups - 1)])
    wait_for(send_sem, 5, part_got.at[others])
    wait_for(send_sem, 6, total_got.at[others])


def body(count, groups, saved_input, out_grad, filters, adapter_down, adapter_up):
    width, tokens = saved_input.shape[1], filters.shape[2]
    ranks = adapter_down.shape[0]
    tables = [jnp.asarray(t) for t in make_tables(count)]
    rows = count * CHANS
    hbm = pl.BlockSpec(memory_space=pl.ANY)
    vmem = pl.BlockSpec(memory_space=pltpu.VMEM)
    spec = pltpu.VMEM((rows, 2 * LANES), F32)
    small = pltpu.VMEM((ranks, LANES), F32)
    some = pltpu.VMEM((groups, ranks, LANES), F32)
    tile = pltpu.VMEM((count, 8, LANES), F32)
    narrow = pltpu.VMEM((rows, LANES), BF16)
    wide = pltpu.VMEM((rows, LANES), F32)
    got = pltpu.VMEM((count, CHANS, LANES), BF16)
    grad_input, grad_filter, down, up = pl.pallas_call(
        functools.partial(kernel, count, groups, float(tokens) ** -0.5),
        out_shape=(
            jax.ShapeDtypeStruct((width, LANES), BF16),
            jax.ShapeDtypeStruct((CHANS, tokens), F32),
            jax.ShapeDtypeStruct((ranks, width), F32),
            jax.ShapeDtypeStruct((ranks, width), F32),
        ),
        in_specs=[hbm, hbm, hbm] + [vmem] * 8,
        out_specs=(hbm, hbm, vmem, vmem),
        scratch_shapes=[
            narrow, wide, narrow, narrow, narrow, got, got, narrow, wide, wide, wide,
            spec, spec, small, some, small, some, tile, tile,
            pltpu.VMEM((8, LANES), F32), tile,
            pltpu.SemaphoreType.DMA((5,)),
            pltpu.SemaphoreType.DMA((7,)),
            pltpu.SemaphoreType.DMA((7,)),
        ],
        compiler_params=pltpu.CompilerParams(
            collective_id=0, has_side_effects=True, vmem_limit_bytes=56 * 1024 * 1024
        ),
    )(saved_input[0], out_grad[0], filters[0], adapter_down[:, 0, :], adapter_up[:, 0, :], *tables)
    return grad_input[None], grad_filter[None], down[:, None, :], up[:, None, :]


def solution(mesh):
    placed = (
        P("grp", None, "ctx"),
        P("grp", None, "ctx"),
        P("grp", "ctx", None),
        P(None, "grp", None),
        P(None, "grp", None),
    )
    return jax.shard_map(
        functools.partial(body, mesh.shape["ctx"], mesh.shape["grp"]),
        mesh=mesh,
        in_specs=placed,
        out_specs=(
            P("grp", None, "ctx"),
            P("grp", "ctx", None),
            P(None, "grp", None),
            P(None, "grp", None),
        ),
        check_vma=False,
    )
```

time: 640 us -> 68.2 us (0.11)
  waiting for transfers between devices: 516 us -> 0 us
  Pallas kernels: 0 us -> 61 us
  matrix products: 47.1 us -> 0 us
  starting transfers between devices: 23.5 us -> 0 us
  blocking collectives: 17.6 us -> 0 us
  between operations: 14.6 us -> 0.65 us
  other arithmetic: 7.43 us -> 0 us
    psum x1 -> x0, waiting for transfers between devices: 499 us -> none  [body(): down_sum, up_sum = lax.psum((down_part, up_part), 'ctx')]
    pallas_call x0 -> x1, Pallas kernels: none -> 61 us  [body(): pl.pallas_call(functools.partial(kernel, count, groups, float(tokens) **...]
    dot_general x18 -> x0, matrix products: 47.1 us -> none  [the longest x3 21.9 us: forward_dft(): spectrum = jnp.einsum('jq,ckq->cjk', second_fwd, joined, precision=HIGH)]
    all_to_all x3 -> x0, starting transfers between devices: 23.5 us -> none  [the longest x1 10.5 us: body(): lax.all_to_all(tok_grad, 'ctx', split_axis=0, concat_axis=1, tiled=True)]
    psum x1 -> x0, blocking collectives: 17.6 us -> none  [body(): lax.psum(jnp.einsum('rc,ct->rt', up_float, du_float, precision=HIGH), 'grp')]
    all_to_all x3 -> x0, waiting for transfers between devices: 17.1 us -> none  [the longest x1 12.4 us: body(): lax.all_to_all(chan_du, 'ctx', split_axis=1, concat_axis=0, tiled=True)]
  transfers between devices with their start and end apart: 4 -> 0, of which waited for: 3 -> 0; matrix products, arithmetic and copies ran while one was open for 2% -> 0% of each run, Pallas kernels for 0% -> 0%
where the time goes in v1:
time: 68.2 us; the launch traced here: 68 us
  Pallas kernels  61 us (89%)
  local copies, waits for them, and re-layouts  6.32 us (9%)
    pallas_call x1, Pallas kernels, body(): pl.pallas_call(functools.partial(kernel, count, groups, float(tokens) **...  61 us
    unnamed x6, local copies, waits for them, and re-layouts  6.32 us

profile of v1, /device:TPU:1, one launch (start us, length us, event | category | flops | bytes accessed | tf_op | source)
XLA Modules:
  0.0 68.0 jit_solution(16024983359904239049)
XLA Ops:
  0.6 61.0 %shard_map.138 = (bf16[2048,128]{1,0:T(8,128)(2,1)}, f32[32,8192]{1,0:T(8,128)}, f32[16,2048]{1,0:T(8,128)}, f32[16,2048]{1,0:T(8,128)}) custom-call(bf16[2048,128]{1,0:T(8,128)(2,1)} %bitcast.11, bf16[2048,128]{1,0:T(8,128)(2,1)} %bitcast.12, f32[32,8192]{1,0:T(8,128)} %bitcast.9, bf16[16,2048]{1,0:T(8,128)(2,1)} %bitcast.16, bf16[16,2048]{1,0:T(8,128)(2,1)} %bitcast.17, ...), custom_call_target="tpu_custom_call" | custom-call | tf_op jit(solution)/shard_map/pallas_call | solution.py:343
  61.6 0.0 copy-start
  61.7 1.8 %copy.15 = f32[16,1,2048]{2,1,0:T(1,128)} copy(f32[16,1,2048]{2,0,1:T(8,128)} %bitcast.15) | data formatting | bytes 262144
  63.4 1.7 %copy.16 = f32[16,1,2048]{2,1,0:T(1,128)} copy(f32[16,1,2048]{2,0,1:T(8,128)} %bitcast.14) | data formatting | bytes 262144
  65.1 1.9 %copy.19 = bf16[1,2048,128]{2,1,0:T(8,128)(2,1)} copy(bf16[1,2048,128]{2,1,0:T(8,128)(2,1)} %bitcast.13) | data formatting | bytes 1048576
  67.0 0.0 copy-done
  67.0 1.0 %copy.20 = f32[1,32,8192]{2,1,0:T(8,128)} copy(f32[1,32,8192]{2,1,0:T(8,128)S(1)} %bitcast.10) | data formatting | bytes 2097152
Async XLA Ops:
  61.6 5.4 %copy-start = (f32[32,8192]{1,0:T(8,128)S(1)}, f32[32,8192]{1,0:T(8,128)}, u32[]{:S(2)}) copy-start(f32[32,8192]{1,0:T(8,128)} %get-tuple-element.9) | copy-start | bytes 3145732

commit v2 on v1

v2 whole, which is shorter than its diff:
```python
import functools
import math

import jax
import jax.numpy as jnp
import numpy as np
from jax import lax
from jax.experimental import pallas as pl
from jax.experimental.pallas import tpu as pltpu
from jax.sharding import PartitionSpec as P

MESH = pl.DeviceIdType.MESH
F32 = jnp.float32
BF16 = jnp.bfloat16
LANES = 128
CHANS = 32
STEP = 8
CHUNK = 16
CHUNKS = CHANS // CHUNK
EARLY = CHUNKS // 2
DY, U, DU = 4, 4 + CHUNKS, 4 + 2 * CHUNKS
GRID = {64: (4, 4, 2, 2), 8: (2, 2, 1, 2)}
VMEM_LIMIT = 56 * 1024 * 1024
SOURCE = pl.ANY


def halves(table):
    high = table.astype(BF16)
    low = (table - high.astype(np.float64)).astype(BF16)
    return high, low


def make_tables(rows):
    points = 2 * rows * LANES
    n = np.arange(rows)
    p = np.arange(LANES)
    theta = np.outer(n + 0.5, n) * (2.0 * math.pi / (2 * rows))
    phi = np.outer(p, p) * (2.0 * math.pi / LANES)
    turn = np.outer(n + 0.5, p) * (2.0 * math.pi / points)
    high, low = halves(np.concatenate([np.cos(theta), -np.sin(theta)], axis=0))
    first_two = np.concatenate([high, low], axis=1)
    first_three = np.concatenate([high, high, low], axis=1)
    cos, sin = np.cos(phi), np.sin(phi)
    high, low = halves(np.block([[cos, -sin], [sin, cos]]))
    second = np.concatenate([high, high, low], axis=0)
    high, low = halves(np.block([[cos, sin], [-sin, cos]]))
    third = np.concatenate([high, high, low], axis=0)
    high, low = halves(np.concatenate([np.cos(theta).T, -np.sin(theta).T], axis=1) * (2.0 / points))
    last = np.concatenate([high, high, low], axis=1)
    twist = np.stack([np.cos(turn), np.sin(turn)]).astype(np.float32)
    return first_two, first_three, twist, second, third, last


def split(value):
    high = value.astype(BF16)
    return high, (value - high.astype(F32)).astype(BF16)


def dot(left, right, dims=((1,), (0,))):
    return lax.dot_general(left, right, (dims, ((), ())), preferred_element_type=F32)


def gather_rows(ref, first, rows):
    blocks = [ref[pl.ds(first + j, rows, stride=CHANS), :] for j in range(STEP)]
    return jnp.concatenate(blocks, axis=1)


def forward(data, first, twist, second, exact):
    rows = data.shape[0]
    if exact:
        narrow = data.astype(BF16)
        stacked = jnp.concatenate([narrow, narrow], axis=0)
    else:
        high, low = split(data)
        stacked = jnp.concatenate([high, low, high], axis=0)
    part = dot(first[...], stacked)
    cos, sin = twist[0], twist[1]
    joined = []
    for j in range(STEP):
        lanes = slice(j * LANES, (j + 1) * LANES)
        real, imag = part[:rows, lanes], part[rows:, lanes]
        joined.append(jnp.concatenate([real * cos + imag * sin, imag * cos - real * sin], axis=1))
    high, low = split(jnp.concatenate(joined, axis=0))
    return dot(jnp.concatenate([high, low, high], axis=1), second[...])


def inverse(spectrum, twist, third, last):
    rows = twist.shape[1]
    high, low = split(spectrum)
    part = dot(jnp.concatenate([high, low, high], axis=1), third[...])
    cos, sin = twist[0], twist[1]
    reals, imags = [], []
    for j in range(STEP):
        real = part[j * rows : (j + 1) * rows, :LANES]
        imag = part[j * rows : (j + 1) * rows, LANES:]
        reals.append(real * cos - imag * sin)
        imags.append(real * sin + imag * cos)
    joined = jnp.concatenate([jnp.concatenate(reals, axis=1), jnp.concatenate(imags, axis=1)], axis=0)
    high, low = split(joined)
    return dot(last[...], jnp.concatenate([high, low, high], axis=0))


def conj_product(left, right):
    lr, li = left[:, :LANES], left[:, LANES:]
    rr, ri = right[:, :LANES], right[:, LANES:]
    return jnp.concatenate([lr * rr + li * ri, li * rr - lr * ri], axis=1)


def kernel(
    count, groups, factor,
    x_hbm, dy_hbm, h_hbm, a_hbm, b_hbm, first_two_hbm, first_three_hbm, twist_hbm, second_hbm, third_hbm, last_hbm,
    gi_hbm, gf_hbm, gd_hbm, gu_hbm,
    a_ref, b_ref, first_two, first_three, twist, second, third, last,
    x_buf, h_buf, u_buf, du_buf, gi_buf, dy_got, u_got, du_got, wide, work, gf_buf,
    spec_h, spec_dy, z_mine, z_got, r_mine, r_got, parts, part_got, total, total_got,
    load_sem, send_sem, recv_sem,
):
    me = lax.axis_index("ctx")
    grp = lax.axis_index("grp")
    high, wide_x, deep, cores = GRID[count]
    core, near = me % cores, me % (deep * cores) // cores
    place = me // (deep * cores)
    down, across = place // wide_x, place % wide_x
    width = count * CHANS
    ranks = a_ref.shape[0]
    inner = [
        ((near + k // cores) % deep) * cores + (core + k % cores) % cores for k in range(deep * cores)
    ]
    sides = [((near + k) % deep) * cores for k in range(deep)]

    def chip(i):
        return (((down + i // wide_x) % high) * wide_x + (across + i % wide_x) % wide_x) * (deep * cores)

    def each_peer(action):
        for k in range(1, deep * cores):
            action(place * deep * cores + inner[k])

        def run(i, carry):
            base = chip(i)
            for offset in inner:
                action(base + offset)
            return carry

        lax.fori_loop(1, high * wide_x, run, 0)

    def each_owner(role, action):
        @pl.when(core != role)
        def _():
            action(place * deep * cores + sides[0] + role)

        for side in sides[1:]:
            action(place * deep * cores + side + role)

        def run(i, carry):
            base = chip(i)
            for side in sides:
                action(base + side + role)
            return carry

        lax.fori_loop(1, high * wide_x, run, 0)

    def each_group(action):
        for e in range(1, groups):
            action(lax.rem(grp + e, groups))

    def send(src, dst, slot, target):
        pltpu.make_async_remote_copy(
            src_ref=src, dst_ref=dst, send_sem=send_sem.at[slot], recv_sem=recv_sem.at[slot],
            device_id=target, device_id_type=MESH,
        ).start()

    def wait_for(sems, slot, ref):
        pltpu.make_async_copy(ref, ref, sems.at[slot]).wait()

    def rows_of(n, size):
        return pl.ds(pl.multiple_of(n * size, size), size)

    def lanes_of(n):
        return pl.ds(pl.multiple_of(n * LANES, LANES), LANES)

    def chunk_rows(p, q):
        return pl.ds(pl.multiple_of(p * CHANS + q * CHUNK, CHUNK), CHUNK)

    barrier = pltpu.get_barrier_semaphore()

    def greet(target):
        pl.semaphore_signal(barrier, inc=1, device_id=target, device_id_type=MESH)

    each_peer(lambda p: greet({"ctx": p}))
    each_group(lambda g: greet({"grp": g}))

    loads = [
        pltpu.make_async_copy(src, dst, load_sem.at[k])
        for k, (src, dst) in enumerate(
            [
                (a_hbm, a_ref), (x_hbm, x_buf), (first_three_hbm, first_three), (twist_hbm, twist),
                (second_hbm, second), (b_hbm, b_ref), (first_two_hbm, first_two), (third_hbm, third),
                (last_hbm, last),
            ]
        )
    ]
    for load in loads:
        load.start()

    def load_h(n, carry):
        pltpu.make_async_copy(h_hbm.at[:, lanes_of(n)], h_buf.at[rows_of(n, CHANS)], load_sem.at[9]).start()
        return carry

    lax.fori_loop(0, count, load_h, 0)
    own = [
        pltpu.make_async_copy(dy_hbm.at[chunk_rows(me, q)], dy_got.at[q, me], load_sem.at[12 + q])
        for q in range(CHUNKS)
    ]
    for copy in own:
        copy.start()
    loads[0].wait()
    loads[1].wait()
    z_mine[...] = dot(a_ref[...], x_buf[...])
    pl.semaphore_wait(barrier, count - 1 + groups - 1)

    each_group(lambda g: send(z_mine, z_got.at[grp], 0, {"grp": g}))
    for q in range(CHUNKS):
        each_peer(lambda p: send(dy_hbm.at[chunk_rows(p, q)], dy_got.at[q, me], DY + q, {"ctx": p}))

    pltpu.make_async_copy(h_buf, h_buf, load_sem.at[9]).wait()
    for load in loads[2:]:
        load.wait()

    def spectrum_h(i, carry):
        data = gather_rows(h_buf, i * STEP, count)
        spec_h[rows_of(i, STEP * count), :] = forward(data, first_three, twist, second, False)
        return carry

    lax.fori_loop(0, CHANS // STEP, spectrum_h, 0)

    def shared_sum(mine, got):
        got[grp] = mine[...]
        acc = got[0]
        for g in range(1, groups):
            acc = acc + got[g]
        return acc

    def low_rank(base, maps, value, out):
        high_part, low_part = split(value)
        pair = jnp.concatenate([high_part, low_part], axis=0)
        chunk = 256
        for start in range(0, width, chunk):
            left = maps[:, start : start + chunk]
            left = jnp.concatenate([left, left], axis=0)
            extra = dot(left, pair, ((0,), (0,)))
            out[start : start + chunk, :] = (base(start, chunk).astype(F32) + extra).astype(BF16)

    wait_for(recv_sem, 0, z_got.at[pl.ds(0, groups - 1)])
    z = shared_sum(z_mine, z_got)
    low_rank(lambda s, n: x_buf[s : s + n, :], b_ref, z, u_buf)
    for q in range(CHUNKS):
        u_got[q, me] = u_buf[chunk_rows(me, q), :]

    def send_u(q):
        each_peer(lambda p: send(u_buf.at[chunk_rows(p, q)], u_got.at[q, me], U + q, {"ctx": p}))

    for q in range(EARLY):
        send_u(q)

    others = pl.ds(0, count - 1)

    def widen(got, q):
        def run(n, carry):
            wide[chunk_rows(n, q), :] = got[q, n].astype(F32)
            return carry

        lax.fori_loop(0, count, run, 0, unroll=8)

    def scatter_rows(ref, first, value):
        for j in range(STEP):
            ref[pl.ds(first + j, count, stride=CHANS), :] = value[:, j * LANES : (j + 1) * LANES]

    def conv_grad(i, carry):
        rows = rows_of(i, STEP * count)
        spec = forward(gather_rows(wide, i * STEP, count), first_two, twist, second, True)
        spec_dy[rows, :] = spec
        scatter_rows(work, i * STEP, inverse(conj_product(spec, spec_h[rows, :]), twist, third, last))
        return carry

    steps = CHUNK // STEP
    for q in range(CHUNKS):
        own[q].wait()
        wait_for(recv_sem, DY + q, dy_got.at[q, others])
        widen(dy_got, q)
        lax.fori_loop(q * steps, (q + 1) * steps, conv_grad, 0)

        def narrow(n, carry):
            du_buf[chunk_rows(n, q), :] = work[chunk_rows(n, q), :].astype(BF16)
            return carry

        lax.fori_loop(0, count, narrow, 0, unroll=8)
        du_got[chunk_rows(me, q), :] = du_buf[chunk_rows(me, q), :]
        each_peer(lambda p: send(du_buf.at[chunk_rows(p, q)], du_got.at[chunk_rows(me, q)], DU + q, {"ctx": p}))
    for q in range(EARLY, CHUNKS):
        send_u(q)

    def filter_grad(i, carry):
        rows = rows_of(i, STEP * count)
        spec = forward(gather_rows(wide, i * STEP, count), first_two, twist, second, True)
        scatter_rows(gf_buf, i * STEP, inverse(conj_product(spec_dy[rows, :], spec), twist, third, last))
        return carry

    def filter_chunk(q):
        wait_for(recv_sem, U + q, u_got.at[q, others])
        widen(u_got, q)
        lax.fori_loop(q * steps, (q + 1) * steps, filter_grad, 0)

    for q in range(EARLY):
        filter_chunk(q)

    for q in range(CHUNKS):
        wait_for(recv_sem, DU + q, dy_got.at[q, others])
    r_mine[...] = dot(b_ref[...], du_got[...])
    each_group(lambda g: send(r_mine, r_got.at[grp], 1, {"grp": g}))

    blocks = width // LANES
    half = ranks * blocks

    def outer(value, tokens, offset):
        first, rest = split(value)
        both = dot(jnp.concatenate([first, rest], axis=0), tokens, ((1,), (1,)))
        out = (both[:ranks] + both[ranks:]) * factor
        for k in range(blocks):
            parts[pl.ds(offset + k, ranks, stride=blocks), :] = out[:, k * LANES : (k + 1) * LANES]

    def tile_of(p):
        return rows_of(p % 2 * (count // 2) + p // 2, 8)

    def send_parts(role):
        each_owner(role, lambda p: send(parts.at[tile_of(p)], part_got.at[me], 2, {"ctx": p}))

    outer(z, du_got[...], half)
    send_parts(1)
    wait_for(recv_sem, 1, r_got.at[pl.ds(0, groups - 1)])
    rank_grad = shared_sum(r_mine, r_got)
    outer(rank_grad, x_buf[...], 0)
    send_parts(0)
    part_got[me] = parts[tile_of(me), :]
    low_rank(lambda s, n: du_got[s : s + n, :], a_ref, rank_grad, gi_buf)
    gi_store = pltpu.make_async_copy(gi_buf, gi_hbm, load_sem.at[10])
    gi_store.start()

    for q in range(EARLY, CHUNKS):
        filter_chunk(q)

    def store_gf(n, carry):
        pltpu.make_async_copy(gf_buf.at[rows_of(n, CHANS)], gf_hbm.at[:, lanes_of(n)], load_sem.at[11]).start()
        return carry

    lax.fori_loop(0, count, store_gf, 0)

    wait_for(recv_sem, 2, part_got.at[others])
    acc = jnp.sum(part_got[...], axis=0)
    total[...] = acc
    total_got[tile_of(me), :] = acc
    each_peer(lambda p: send(total, total_got.at[tile_of(me)], 3, {"ctx": p}))
    wait_for(recv_sem, 3, part_got.at[others])
    stores = [
        pltpu.make_async_copy(total_got.at[pl.ds(0, half)], gd_hbm, load_sem.at[0]),
        pltpu.make_async_copy(total_got.at[pl.ds(half, half)], gu_hbm, load_sem.at[1]),
    ]
    for store in stores:
        store.start()

    gi_store.wait()
    pltpu.make_async_copy(gf_buf, gf_buf, load_sem.at[11]).wait()
    for slot in range(2):
        wait_for(send_sem, slot, z_got.at[pl.ds(0, groups - 1)])
    for slot in range(2, 4):
        wait_for(send_sem, slot, part_got.at[others])
    for slot in range(DY, DY + 3 * CHUNKS):
        wait_for(send_sem, slot, dy_got.at[0, others])
    for store in stores:
        store.wait()


def body(count, groups, saved_input, out_grad, filters, adapter_down, adapter_up):
    width, tokens = saved_input.shape[1], filters.shape[2]
    ranks = adapter_down.shape[0]
    tables = [jnp.asarray(t) for t in make_tables(count)]
    rows = count * CHANS
    hbm = pl.BlockSpec(memory_space=pl.ANY)
    source = pl.BlockSpec(memory_space=SOURCE)
    spec = pltpu.VMEM((rows, 2 * LANES), F32)
    small = pltpu.VMEM((ranks, LANES), F32)
    some = pltpu.VMEM((groups, ranks, LANES), F32)
    narrow = pltpu.VMEM((rows, LANES), BF16)
    wide = pltpu.VMEM((rows, LANES), F32)
    maps = pltpu.VMEM((ranks, width), BF16)
    tiles = pltpu.VMEM((count * 8, LANES), F32)
    got = pltpu.VMEM((CHUNKS, count, CHUNK, LANES), BF16)
    flat = ranks * width // LANES
    grad_input, grad_filter, down, up = pl.pallas_call(
        functools.partial(kernel, count, groups, float(tokens) ** -0.5),
        out_shape=(
            jax.ShapeDtypeStruct((width, LANES), BF16),
            jax.ShapeDtypeStruct((CHANS, tokens), F32),
            jax.ShapeDtypeStruct((flat, LANES), F32),
            jax.ShapeDtypeStruct((flat, LANES), F32),
        ),
        in_specs=[source] * 11,
        out_specs=(hbm,) * 4,
        scratch_shapes=[
            maps, maps, *[pltpu.VMEM(t.shape, t.dtype) for t in tables],
            narrow, wide, narrow, narrow, narrow, got, got, narrow, wide, wide, wide,
            spec, spec, small, some, small, some, tiles, pltpu.VMEM((count, 8, LANES), F32),
            pltpu.VMEM((8, LANES), F32), tiles,
            pltpu.SemaphoreType.DMA((12 + CHUNKS,)),
            pltpu.SemaphoreType.DMA((4 + 3 * CHUNKS,)),
            pltpu.SemaphoreType.DMA((4 + 3 * CHUNKS,)),
        ],
        compiler_params=pltpu.CompilerParams(
            collective_id=0, has_side_effects=True, vmem_limit_bytes=VMEM_LIMIT
        ),
    )(saved_input[0], out_grad[0], filters[0], adapter_down[:, 0, :], adapter_up[:, 0, :], *tables)
    return (
        grad_input[None],
        grad_filter[None],
        down.reshape(ranks, 1, width),
        up.reshape(ranks, 1, width),
    )


def solution(mesh):
    placed = (
        P("grp", None, "ctx"),
        P("grp", None, "ctx"),
        P("grp", "ctx", None),
        P(None, "grp", None),
        P(None, "grp", None),
    )
    return jax.shard_map(
        functools.partial(body, mesh.shape["ctx"], mesh.shape["grp"]),
        mesh=mesh,
        in_specs=placed,
        out_specs=(
            P("grp", None, "ctx"),
            P("grp", "ctx", None),
            P(None, "grp", None),
            P(None, "grp", None),
        ),
        check_vma=False,
    )
```

time: 68.2 us -> 56.3 us (0.83)
  Pallas kernels: 61 us -> 50.9 us
  local copies, waits for them, and re-layouts: 6.32 us -> 4.59 us
    pallas_call x1, Pallas kernels: 61 us -> 50.9 us  [body(): pl.pallas_call(functools.partial(kernel, count, groups, float(tokens) **...]
    unnamed x6 -> x10, local copies, waits for them, and re-layouts: 6.32 us -> 4.59 us
where the time goes in v2:
time: 56.3 us; the launch traced here: 56.1 us
  Pallas kernels  50.9 us (90%)
  local copies, waits for them, and re-layouts  4.59 us (8%)
  between operations  0.65 us (1%)
    pallas_call x1, Pallas kernels, body(): pl.pallas_call(functools.partial(kernel, count, groups, float(tokens) **...  50.9 us
    unnamed x10, local copies, waits for them, and re-layouts  4.59 us

profile of v2, /device:TPU:1, one launch (start us, length us, event | category | flops | bytes accessed | tf_op | source)
XLA Modules:
  0.0 56.1 jit_solution(5890241898073175239)
XLA Ops:
  0.6 50.9 %shard_map.138 = (bf16[2048,128]{1,0:T(8,128)(2,1)}, f32[32,8192]{1,0:T(8,128)}, f32[256,128]{1,0:T(8,128)}, f32[256,128]{1,0:T(8,128)}) custom-call(bf16[2048,128]{1,0:T(8,128)(2,1)} %bitcast.11, bf16[2048,128]{1,0:T(8,128)(2,1)} %bitcast.12, f32[32,8192]{1,0:T(8,128)} %bitcast.9, bf16[16,2048]{1,0:T(8,128)(2,1)} %bitcast.16, bf16[16,2048]{1,0:T(8,128)(2,1)} %bitcast.17, ...), custom_call_target="tpu_custom_call" | custom-call | tf_op jit(solution)/shard_map/pallas_call | solution.py:398
  51.5 0.0 copy-start
  51.5 2.0 %copy.21 = bf16[1,2048,128]{2,1,0:T(8,128)(2,1)} copy(bf16[1,2048,128]{2,1,0:T(8,128)(2,1)} %bitcast.13) | data formatting | bytes 1048576
  53.5 0.0 copy-done
  53.5 0.0 copy-start.2
  53.5 1.0 %copy.22 = f32[1,32,8192]{2,1,0:T(8,128)} copy(f32[1,32,8192]{2,1,0:T(8,128)S(1)} %bitcast.10) | data formatting | bytes 2097152
  54.5 0.1 copy-done.2
  54.5 0.0 copy-start.1
  54.5 0.7 %copy.23 = f32[16,1,2048]{2,1,0:T(1,128)} copy(f32[16,1,2048]{2,1,0:T(1,128)S(1)} %bitcast.15) | data formatting | bytes 262144
  55.2 0.3 copy-done.1
  55.5 0.7 %copy.24 = f32[16,1,2048]{2,1,0:T(1,128)} copy(f32[16,1,2048]{2,1,0:T(1,128)S(1)} %bitcast.14) | data formatting | bytes 262144
Async XLA Ops:
  51.5 2.0 %copy-start = (f32[32,8192]{1,0:T(8,128)S(1)}, f32[32,8192]{1,0:T(8,128)}, u32[]{:S(2)}) copy-start(f32[32,8192]{1,0:T(8,128)} %get-tuple-element.9) | copy-start | bytes 3145732
  53.5 1.0 %copy-start.2 = (f32[256,128]{1,0:T(8,128)S(1)}, f32[256,128]{1,0:T(8,128)}, u32[]{:S(2)}) copy-start(f32[256,128]{1,0:T(8,128)} %get-tuple-element.10) | copy-start | bytes 393220
  54.5 1.0 %copy-start.1 = (f32[256,128]{1,0:T(8,128)S(1)}, f32[256,128]{1,0:T(8,128)}, u32[]{:S(2)}) copy-start(f32[256,128]{1,0:T(8,128)} %get-tuple-element.11) | copy-start | bytes 393220

commit v3 on v2

--- a/solution.py
+++ b/solution.py
@@ -18,10 +18,24 @@
 CHUNK = 16
 CHUNKS = CHANS // CHUNK
 EARLY = CHUNKS // 2
+FAR = True
 DY, U, DU = 4, 4 + CHUNKS, 4 + 2 * CHUNKS
 GRID = {64: (4, 4, 2, 2), 8: (2, 2, 1, 2)}
 VMEM_LIMIT = 56 * 1024 * 1024
 SOURCE = pl.ANY
+
+
+def far_first(high, wide, direct):
+    def hops(i):
+        down, across = i // wide, i % wide
+        return min(down, high - down) + min(across, wide - across)
+
+    order = sorted(range(1, high * wide), key=lambda i: (-hops(i), i) if direct else i)
+    late = [k for k, i in enumerate(order[:8]) if i < 8]
+    if len(order) > 8:
+        order.insert(7, order.pop(late[-1]))
+    codes = [sum(i << (4 * k) for k, i in enumerate(part)) for part in (order[:8], order[8:])]
+    return len(order), codes
 
 
 def halves(table):
@@ -109,9 +123,9 @@
 def kernel(
     count, groups, factor,
     x_hbm, dy_hbm, h_hbm, a_hbm, b_hbm, first_two_hbm, first_three_hbm, twist_hbm, second_hbm, third_hbm, last_hbm,
-    gi_hbm, gf_hbm, gd_hbm, gu_hbm,
+    gi_ref, gf_ref, gd_ref, gu_ref,
     a_ref, b_ref, first_two, first_three, twist, second, third, last,
-    x_buf, h_buf, u_buf, du_buf, gi_buf, dy_got, u_got, du_got, wide, work, gf_buf,
+    x_buf, h_buf, u_buf, du_buf, dy_got, u_got, du_got, wide, work, gf_buf,
     spec_h, spec_dy, z_mine, z_got, r_mine, r_got, parts, part_got, total, total_got,
     load_sem, send_sem, recv_sem,
 ):
@@ -121,43 +135,47 @@
     core, near = me % cores, me % (deep * cores) // cores
     place = me // (deep * cores)
     down, across = place // wide_x, place % wide_x
+    chips, codes = far_first(high, wide_x, FAR)
     width = count * CHANS
     ranks = a_ref.shape[0]
     inner = [
-        ((near + k // cores) % deep) * cores + (core + k % cores) % cores for k in range(deep * cores)
+        ((near + k // cores) % deep) * cores + (core + k % cores) % cores
+        for k in reversed(range(deep * cores))
     ]
-    sides = [((near + k) % deep) * cores for k in range(deep)]
-
-    def chip(i):
-        return (((down + i // wide_x) % high) * wide_x + (across + i % wide_x) % wide_x) * (deep * cores)
+    sides = [((near + k) % deep) * cores for k in reversed(range(deep))]
+
+    def chip(t):
+        code = jnp.where(t < 8, codes[0], codes[1])
+        i = (code >> (4 * (t & 7))) & 15
+        row = (down + i // wide_x if wide_x != 4 else down + (i >> 2)) & (high - 1)
+        column = (across + i) & (wide_x - 1)
+        return (row * wide_x + column) * (deep * cores)
 
     def each_peer(action):
-        for k in range(1, deep * cores):
-            action(place * deep * cores + inner[k])
-
-        def run(i, carry):
-            base = chip(i)
+        def run(t, carry):
+            base = chip(t)
             for offset in inner:
                 action(base + offset)
             return carry
 
-        lax.fori_loop(1, high * wide_x, run, 0)
+        lax.fori_loop(0, chips, run, 0)
+        for offset in inner[:-1]:
+            action(place * deep * cores + offset)
 
     def each_owner(role, action):
-        @pl.when(core != role)
-        def _():
-            action(place * deep * cores + sides[0] + role)
-
-        for side in sides[1:]:
-            action(place * deep * cores + side + role)
-
-        def run(i, carry):
-            base = chip(i)
+        def run(t, carry):
+            base = chip(t)
             for side in sides:
                 action(base + side + role)
             return carry
 
-        lax.fori_loop(1, high * wide_x, run, 0)
+        lax.fori_loop(0, chips, run, 0)
+        for side in sides[:-1]:
+            action(place * deep * cores + side + role)
+
+        @pl.when(core != role)
+        def _():
+            action(place * deep * cores + sides[-1] + role)
 
     def each_group(action):
         for e in range(1, groups):
@@ -341,33 +359,26 @@
     outer(rank_grad, x_buf[...], 0)
     send_parts(0)
     part_got[me] = parts[tile_of(me), :]
-    low_rank(lambda s, n: du_got[s : s + n, :], a_ref, rank_grad, gi_buf)
-    gi_store = pltpu.make_async_copy(gi_buf, gi_hbm, load_sem.at[10])
-    gi_store.start()
+    low_rank(lambda s, n: du_got[s : s + n, :], a_ref, rank_grad, gi_ref)
 
     for q in range(EARLY, CHUNKS):
         filter_chunk(q)
-
-    def store_gf(n, carry):
-        pltpu.make_async_copy(gf_buf.at[rows_of(n, CHANS)], gf_hbm.at[:, lanes_of(n)], load_sem.at[11]).start()
-        return carry
-
-    lax.fori_loop(0, count, store_gf, 0)
-
     wait_for(recv_sem, 2, part_got.at[others])
     acc = jnp.sum(part_got[...], axis=0)
     total[...] = acc
     total_got[tile_of(me), :] = acc
     each_peer(lambda p: send(total, total_got.at[tile_of(me)], 3, {"ctx": p}))
+
+    def store_gf(n, carry):
+        pltpu.make_async_copy(gf_buf.at[rows_of(n, CHANS)], gf_ref.at[:, lanes_of(n)], load_sem.at[11]).start()
+        return carry
+
+    lax.fori_loop(0, count, store_gf, 0)
+
     wait_for(recv_sem, 3, part_got.at[others])
-    stores = [
-        pltpu.make_async_copy(total_got.at[pl.ds(0, half)], gd_hbm, load_sem.at[0]),
-        pltpu.make_async_copy(total_got.at[pl.ds(half, half)], gu_hbm, load_sem.at[1]),
-    ]
-    for store in stores:
-        store.start()
-
-    gi_store.wait()
+    gd_ref[...] = total_got[pl.ds(0, half), :]
+    gu_ref[...] = total_got[pl.ds(half, half), :]
+
     pltpu.make_async_copy(gf_buf, gf_buf, load_sem.at[11]).wait()
     for slot in range(2):
         wait_for(send_sem, slot, z_got.at[pl.ds(0, groups - 1)])
@@ -375,8 +386,17 @@
         wait_for(send_sem, slot, part_got.at[others])
     for slot in range(DY, DY + 3 * CHUNKS):
         wait_for(send_sem, slot, dy_got.at[0, others])
-    for store in stores:
-        store.wait()
+
+
+def store_kernel(gi, gf, gd, gu, gi_out, gf_out, gd_out, gu_out, sems):
+    copies = [
+        pltpu.make_async_copy(src, dst, sems.at[k])
+        for k, (src, dst) in enumerate([(gf, gf_out), (gi, gi_out), (gd, gd_out), (gu, gu_out)])
+    ]
+    for copy in copies:
+        copy.start()
+    for copy in copies:
+        copy.wait()
 
 
 def body(count, groups, saved_input, out_grad, filters, adapter_down, adapter_up):
@@ -395,19 +415,19 @@
     tiles = pltpu.VMEM((count * 8, LANES), F32)
     got = pltpu.VMEM((CHUNKS, count, CHUNK, LANES), BF16)
     flat = ranks * width // LANES
-    grad_input, grad_filter, down, up = pl.pallas_call(
+    results = pl.pallas_call(
         functools.partial(kernel, count, groups, float(tokens) ** -0.5),
         out_shape=(
-            jax.ShapeDtypeStruct((width, LANES), BF16),
-            jax.ShapeDtypeStruct((CHANS, tokens), F32),
-            jax.ShapeDtypeStruct((flat, LANES), F32),
-            jax.ShapeDtypeStruct((flat, LANES), F32),
+            pltpu.VMEM((width, LANES), BF16),
+            pltpu.VMEM((CHANS, tokens), F32),
+            pltpu.VMEM((flat, LANES), F32),
+            pltpu.VMEM((flat, LANES), F32),
         ),
         in_specs=[source] * 11,
-        out_specs=(hbm,) * 4,
+        out_specs=(pl.BlockSpec(memory_space=pltpu.VMEM),) * 4,
         scratch_shapes=[
             maps, maps, *[pltpu.VMEM(t.shape, t.dtype) for t in tables],
-            narrow, wide, narrow, narrow, narrow, got, got, narrow, wide, wide, wide,
+            narrow, wide, narrow, narrow, got, got, narrow, wide, wide, wide,
             spec, spec, small, some, small, some, tiles, pltpu.VMEM((count, 8, LANES), F32),
             pltpu.VMEM((8, LANES), F32), tiles,
             pltpu.SemaphoreType.DMA((12 + CHUNKS,)),
@@ -418,6 +438,13 @@
             collective_id=0, has_side_effects=True, vmem_limit_bytes=VMEM_LIMIT
         ),
     )(saved_input[0], out_grad[0], filters[0], adapter_down[:, 0, :], adapter_up[:, 0, :], *tables)
+    grad_input, grad_filter, down, up = pl.pallas_call(
+        store_kernel,
+        out_shape=tuple(jax.ShapeDtypeStruct(r.shape, r.dtype) for r in results),
+        in_specs=[pl.BlockSpec(memory_space=pltpu.VMEM)] * 4,
+        out_specs=(hbm,) * 4,
+        scratch_shapes=[pltpu.SemaphoreType.DMA((4,))],
+    )(*[pltpu.with_memory_space_constraint(r, pltpu.VMEM) for r in results])
     return (
         grad_input[None],
         grad_filter[None],

time: 56.3 us -> 49.6 us (0.88)
  local copies, waits for them, and re-layouts: 4.59 us -> 0 us
  Pallas kernels: 50.9 us -> 48.9 us
    unnamed x10 -> x0, local copies, waits for them, and re-layouts: 4.59 us -> none
    pallas_call x1, Pallas kernels: 50.9 us -> 47.6 us  [body(): pl.pallas_call(functools.partial(kernel, count, groups, float(tokens) **...]
    pallas_call x0 -> x1, Pallas kernels: none -> 1.25 us  [body(): pl.pallas_call(store_kernel, out_shape=tuple((jax.ShapeDtypeStruct(r.shap...]
where the time goes in v3:
time: 49.6 us; the launch traced here: 49.5 us
  Pallas kernels  48.9 us (99%)
  between operations  0.64 us (1%)
    pallas_call x1, Pallas kernels, body(): pl.pallas_call(functools.partial(kernel, count, groups, float(tokens) **...  47.6 us
    pallas_call x1, Pallas kernels, body(): pl.pallas_call(store_kernel, out_shape=tuple((jax.ShapeDtypeStruct(r.shap...  1.25 us

profile of v3, /device:TPU:1, one launch (start us, length us, event | category | flops | bytes accessed | tf_op | source)
XLA Modules:
  0.0 49.5 jit_solution(17564627516986838337)
XLA Ops:
  0.6 47.6 %shard_map.138 = (bf16[2048,128]{1,0:T(8,128)(2,1)S(1)}, f32[32,8192]{1,0:T(8,128)S(1)}, f32[256,128]{1,0:T(8,128)S(1)}, f32[256,128]{1,0:T(8,128)S(1)}) custom-call(bf16[2048,128]{1,0:T(8,128)(2,1)} %bitcast.10, bf16[2048,128]{1,0:T(8,128)(2,1)} %bitcast.11, f32[32,8192]{1,0:T(8,128)} %bitcast.9, bf16[16,2048]{1,0:T(8,128)(2,1)} %bitcast.12, ...), custom_call_target="tpu_custom_call" | custom-call | tf_op jit(solution)/shard_map/pallas_call | solution.py:418
  48.3 1.3 %shard_map.139 = (bf16[2048,128]{1,0:T(8,128)(2,1)}, f32[32,8192]{1,0:T(8,128)}, f32[256,128]{1,0:T(8,128)}, f32[256,128]{1,0:T(8,128)}) custom-call(bf16[2048,128]{1,0:T(8,128)(2,1)S(1)} %get-tuple-element.12.gi, f32[32,8192]{1,0:T(8,128)S(1)} %get-tuple-element.13.gf, f32[256,128]{1,0:T(8,128)S(1)} %get-tuple-element.14.gd, ...), custom_call_target="tpu_custom_call" | custom-call | tf_op jit(solution)/shard_map/pallas_call | solution.py:441
